TPU v7x, 32 devices: a whole 2x2x4 slice. The times are simulated.
32 devices in a mesh: group: 2 (over y), patch: 4 (over z), head: 2 (over x), cfg: 2 (over core).
Axes of the slice: x: 2, y: 2, z: 4, core: 2. Of those that a mesh axis runs over, the one named last changes fastest.
Arguments:
- fresh_query: bfloat16 [4, 256, 2560], P(('group', 'cfg'), ('patch', 'head')), parts along dimension 0, may hold values from -32 to 32
- fresh_key: bfloat16 [4, 256, 2560], P(('group', 'cfg'), ('patch', 'head')), parts along dimension 0, may hold values from -9 to 9
- fresh_value: bfloat16 [4, 256, 2560], P(('group', 'cfg'), ('patch', 'head')), parts along dimension 0, may hold values from -12 to 12
- stale_key: bfloat16 [4, 256, 2560], P(('group', 'cfg'), 'patch', 'head'), parts along dimension 0, may hold values from -8 to 8
- stale_value: bfloat16 [4, 256, 2560], P(('group', 'cfg'), 'patch', 'head'), parts along dimension 0, may hold values from -12 to 12
- cross_query: bfloat16 [4, 256, 2560], P(('group', 'cfg'), ('patch', 'head')), parts along dimension 0, may hold values from -32 to 32
- text_key: bfloat16 [4, 512, 2560], P(('group', 'cfg'), None, 'head'), parts along dimension 0, may hold values from -8 to 8
- text_value: bfloat16 [4, 512, 2560], P(('group', 'cfg'), None, 'head'), parts along dimension 0, may hold values from -12 to 12
- text_mask: int32 [4, 512], P(('group', 'cfg')), parts along dimension 0, may hold values from 0 to 1, as said below
Outputs:
- self_mixed: bfloat16 [4, 256, 2560], P(('group', 'cfg'), ('patch', 'head')), parts along dimension 0
- cross_mixed: bfloat16 [4, 256, 2560], P(('group', 'cfg'), ('patch', 'head')), parts along dimension 0
There are 2 independent parts, one for each index of `group`. A program takes and returns all parts, laid end to end along the dimension named above; each array names one. Nothing has to cross between parts.
Inputs may be any that keep to these rules, and one draw needn't show every extreme that they name: In each branch the ones of text_mask form a prefix of 32 or more positions; in one of the two branches all 512 are ones, in the other some are zeros.
All inputs are finite; a program needn't handle non-finite values.
Results may differ from a plain program's by a relative error of at most 0.005.
Values may be sent and summed in bfloat16 or wider, within the bound.
A program may use at most 128 MiB of HBM per device.

v0:
```python
import math

import jax
import jax.numpy as jnp
from jax import lax
from jax.sharding import PartitionSpec as P

HD = 128


def scaled_scores(queries, key_block):
    return jnp.einsum("qhd,khd->qhk", queries, key_block, preferred_element_type=jnp.float32) * (
        1.0 / math.sqrt(HD)
    )


def absorb(running, scores, value_block, keeper):
    run_top, run_total, run_sum = running
    if keeper is None:
        piece_top = jnp.max(scores, axis=-1, keepdims=True)
        new_top = piece_top
        weights = jnp.exp(scores - new_top)
    else:
        piece_top = jnp.max(jnp.where(keeper, scores, -jnp.inf), axis=-1, keepdims=True)
        new_top = jnp.maximum(run_top, piece_top)
        weights = jnp.where(keeper, jnp.exp(jnp.where(keeper, scores, new_top) - new_top), 0.0)
    factor = jnp.exp(run_top - new_top)
    run_total = run_total * factor + jnp.sum(weights, axis=-1, keepdims=True)
    run_sum = run_sum * factor + jnp.einsum(
        "qhk,khd->qhd",
        weights.astype(jnp.bfloat16),
        value_block,
        preferred_element_type=jnp.float32,
    )
    return (new_top, run_total, run_sum)


def masked_mix(queries, key_block, value_block, usable):
    scores = scaled_scores(queries, key_block)
    row_top = jnp.max(jnp.where(usable, scores, -jnp.inf), axis=-1, keepdims=True)
    weights = jnp.where(usable, jnp.exp(jnp.where(usable, scores, row_top) - row_top), 0.0)
    totals = jnp.sum(weights, axis=-1, keepdims=True)
    mixture = jnp.einsum(
        "qhk,khd->qhd",
        weights.astype(jnp.bfloat16),
        value_block,
        preferred_element_type=jnp.float32,
    )
    return mixture / totals


def per_device(
    fresh_query,
    fresh_key,
    fresh_value,
    stale_key,
    stale_value,
    cross_query,
    text_key,
    text_value,
    text_mask,
):
    usable = (text_mask[0] > 0)[None, None, :]
    text_rows = text_key.shape[1]
    token_rows = fresh_query.shape[1]
    local_query, local_key, local_value = (
        lax.all_to_all(fresh_query, "head", split_axis=2, concat_axis=1, tiled=True),
        lax.all_to_all(fresh_key, "head", split_axis=2, concat_axis=1, tiled=True),
        lax.all_to_all(fresh_value, "head", split_axis=2, concat_axis=1, tiled=True),
    )
    patch_rows = local_query.shape[1]
    heads_here = local_query.shape[2] // HD
    queries = local_query.reshape(patch_rows, heads_here, HD)
    own_keys = local_key.reshape(patch_rows, heads_here, HD)
    own_values = local_value.reshape(patch_rows, heads_here, HD)
    own_first = lax.axis_index("patch") * patch_rows
    starting = (
        jnp.full((patch_rows, heads_here, 1), -jnp.inf, jnp.float32),
        jnp.zeros((patch_rows, heads_here, 1), jnp.float32),
        jnp.zeros((patch_rows, heads_here, HD), jnp.float32),
    )
    opening = absorb(starting, scaled_scores(queries, own_keys), own_values, None)
    piece_key = lax.all_gather(stale_key, "patch", axis=1, tiled=True)
    piece_value = lax.all_gather(stale_value, "patch", axis=1, tiled=True)
    row_count = piece_key.shape[1]
    keys_here = piece_key.reshape(row_count, heads_here, HD)
    values_here = piece_value.reshape(row_count, heads_here, HD)
    positions = jnp.arange(row_count, dtype=jnp.int32)
    keeper = ((positions < own_first) | (positions >= own_first + patch_rows))[None, None, :]
    run_top, run_total, run_sum = absorb(
        opening, scaled_scores(queries, keys_here), values_here, keeper
    )
    self_block = (run_sum / run_total).reshape(1, patch_rows, heads_here * HD).astype(jnp.bfloat16)
    all_heads = cross_query.shape[2] // HD
    cross_heads = cross_query.reshape(token_rows, all_heads, HD)
    piece_key, piece_value = lax.all_gather(
        (
            text_key.reshape(1, text_rows, heads_here, HD),
            text_value.reshape(1, text_rows, heads_here, HD),
        ),
        "head",
        axis=2,
        tiled=True,
    )
    mixture = masked_mix(cross_heads, piece_key[0], piece_value[0], usable)
    gathered = mixture.astype(jnp.bfloat16)[None]
    cross_block = gathered.reshape(1, token_rows, all_heads * HD)
    self_mixed = lax.all_to_all(self_block, "head", split_axis=1, concat_axis=2, tiled=True)
    return (self_mixed, cross_block)


def solution(mesh):
    return jax.shard_map(
        per_device,
        mesh=mesh,
        in_specs=(
            P(("group", "cfg"), ("patch", "head"), None),
            P(("group", "cfg"), ("patch", "head"), None),
            P(("group", "cfg"), ("patch", "head"), None),
            P(("group", "cfg"), "patch", "head"),
            P(("group", "cfg"), "patch", "head"),
            P(("group", "cfg"), ("patch", "head"), None),
            P(("group", "cfg"), None, "head"),
            P(("group", "cfg"), None, "head"),
            P(("group", "cfg"), None),
        ),
        out_specs=(
            P(("group", "cfg"), ("patch", "head"), None),
            P(("group", "cfg"), ("patch", "head"), None),
        ),
        check_vma=False,
    )
```

profile of v0, /device:TPU:0, one launch (start us, length us, event | category | flops | bytes accessed | tf_op | source)
XLA Modules:
  0.0 149.4 jit_solution(1958415783337173645)
XLA Ops:
  7.2 1.6 %copy.97 = bf16[1,512,1280]{1,2,0:T(8,128)(2,1)S(1)} copy(bf16[1,512,1280]{2,1,0:T(8,128)(2,1)} %param.15) | data formatting | bytes 2621440 | tf_op args[6]
  8.8 1.5 copy.98
  10.3 0.9 copy-done.5
  11.2 0.9 copy.79
  12.7 14.4 %reduce.2 = bf16[2560,32]{1,0:T(8,128)(2,1)S(1)} reduce(bf16[2560,1,32]{2,1,0:T(2,128)(2,1)S(1)} %bitcast.72, bf16[]{:T(256)} %broadcast.39), dimensions={1}, to_apply=%bitcast.62.reduce_sub_computation | reduce | bytes 327682
  27.1 1.3 reshape.109
  28.4 4.2 %all-to-all-start.1 = ((bf16[2,2,20480]{2,1,0:T(2,128)(2,1)}), bf16[2,2,20480]{2,1,0:T(2,128)(2,1)S(1)}, u32[]{:S(2)}, u32[]{:S(2)}) async-start(bf16[2,2,20480]{2,1,0:T(2,128)(2,1)} %reshape.109), calls=%async_computation.1 | async-start | bytes 327680 | tf_op jit(solution)/shard_map/all_to_all | solution.py:67
  33.3 1.4 copy.101
  34.8 0.9 copy-done.3
  35.7 19.2 %all_gather.12 = bf16[1,256,1280]{2,1,0:T(8,128)(2,1)S(1)} all-gather(bf16[1,64,1280]{2,1,0:T(8,128)(2,1)S(1)} %copy-done.3), channel_id=1, replica_groups=mesh['group'=2,'patch'=4,'head'=2,'cfg'=2] {'patch'}, dimensions={1}, use_global_device_ids=true | all-gather | bytes 819200 | tf_op jit(solution)/shard_map/all_gather | solution.py:83
  54.8 0.9 copy.76
  55.8 14.3 %reduce.3 = bf16[2560,32]{1,0:T(8,128)(2,1)S(1)} reduce(bf16[2560,1,32]{2,1,0:T(2,128)(2,1)S(1)} %bitcast.78, bf16[]{:T(256)} %broadcast.39), dimensions={1}, to_apply=%bitcast.60.reduce_sub_computation | reduce | bytes 327682
  70.1 1.3 reshape.107
  71.4 4.1 %all-to-all-start = ((bf16[2,2,20480]{2,1,0:T(2,128)(2,1)}), bf16[2,2,20480]{2,1,0:T(2,128)(2,1)}, u32[]{:S(2)}, u32[]{:S(2)}) async-start(bf16[2,2,20480]{2,1,0:T(2,128)(2,1)} %reshape.107), calls=%async_computation | async-start | bytes 327680 | tf_op jit(solution)/shard_map/all_to_all | solution.py:68
  75.5 16.1 %all_gather.13 = bf16[1,256,1280]{2,1,0:T(8,128)(2,1)S(1)} all-gather(bf16[1,64,1280]{2,1,0:T(8,128)(2,1)S(1)} %copy-done.4), channel_id=1, replica_groups=mesh['group'=2,'patch'=4,'head'=2,'cfg'=2] {'patch'}, dimensions={1}, use_global_device_ids=true | all-gather | bytes 819200 | tf_op jit(solution)/shard_map/all_gather | solution.py:84
  92.9 0.9 copy.84
  93.8 14.3 %reduce.4 = bf16[2560,32]{1,0:T(8,128)(2,1)S(1)} reduce(bf16[2560,1,32]{2,1,0:T(2,128)(2,1)S(1)} %bitcast.79, bf16[]{:T(256)} %broadcast.39), dimensions={1}, to_apply=%bitcast.64.reduce_sub_computation | reduce | bytes 327682
  108.1 1.3 reshape.111
  109.4 4.3 %all-to-all-start.2 = ((bf16[2,2,20480]{2,1,0:T(2,128)(2,1)}), bf16[2,2,20480]{2,1,0:T(2,128)(2,1)}, u32[]{:S(2)}, u32[]{:S(2)}) async-start(bf16[2,2,20480]{2,1,0:T(2,128)(2,1)} %reshape.111), calls=%async_computation.2 | async-start | bytes 327680 | tf_op jit(solution)/shard_map/all_to_all | solution.py:69
  113.8 1.5 reshape.110
  115.2 0.7 copy.80
  116.2 1.5 reshape.108
  118.6 1.5 reshape.112
  120.1 1.7 %copy.85 = bf16[1,32,2560]{2,1,0:T(8,128)(2,1)} copy(bf16[1,32,2560]{1,0,2:T(2,128)(2,1)S(1)} %bitcast.75) | data formatting | bytes 327680 | tf_op jit(solution)/shard_map/all_to_all | solution.py:69
  121.8 1.0 all_to_all.53
  124.9 1.6 %reduce.5 = bf16[64,1280]{1,0:T(8,128)(2,1)S(1)} reduce(bf16[64,1,1280]{2,1,0:T(2,128)(2,1)S(1)} %bitcast.81, bf16[]{:T(256)} %broadcast.39), dimensions={1}, to_apply=%bitcast.66.reduce_sub_computation | reduce | bytes 327682
  126.5 0.7 reshape.113
  127.2 3.4 %all-to-all-start.3 = ((bf16[2,2,20480]{2,1,0:T(2,128)(2,1)}), bf16[2,2,20480]{2,1,0:T(2,128)(2,1)S(1)}, u32[]{:S(2)}, u32[]{:S(2)}) async-start(bf16[2,2,20480]{2,1,0:T(2,128)(2,1)} %reshape.113), calls=%async_computation.3 | async-start | bytes 327680 | tf_op jit(solution)/shard_map/all_to_all | solution.py:108
  130.7 4.6 %all-to-all-done.3 = bf16[2,2,20480]{2,1,0:T(2,128)(2,1)S(1)} async-done(((bf16[2,2,20480]{2,1,0:T(2,128)(2,1)}), bf16[2,2,20480]{2,1,0:T(2,128)(2,1)S(1)}, u32[]{:S(2)}, u32[]{:S(2)}) %all-to-all-start.3) | async-done | bytes 163872 | tf_op jit(solution)/shard_map/all_to_all | solution.py:108
  136.1 2.8 %select_reduce_fusion = (f32[32,20]{0,1:T(8,128)S(1)}, f32[32,20,512]{2,0,1:T(8,128)S(1)}) fusion(pred[512]{0:T(512)(128)(4,1)S(1)} %compare_reduce_fusion, bf16[32,20,128]{2,1,0:T(8,128)(2,1)S(1)} %reshape.104, bf16[1,512,20,128]{3,1,0,2:T(8,128)(2,1)} %all-gather.3.cloned.1.call-done), kind=kOutput, calls=%fused_computation.7 | convolution fusion | flops 84868480 | bytes 4099072 | tf_op jit(solution)/shard_map/qhd,khd->qhk/dot_general | solution.py:12
  139.4 2.3 %fusion.23 = bf16[32,20,128]{2,0,1:T(8,128)(2,1)S(1)} fusion(bf16[1,512,20,128]{3,1,0,2:T(8,128)(2,1)} %all-gather.5.cloned.1.call-done, f32[32,20,512]{2,0,1:T(8,128)S(1)} %get-tuple-element.10, f32[32,20]{0,1:T(8,128)S(1)} %get-tuple-element.9, pred[512]{0:T(512)(128)(4,1)S(1)} %compare_reduce_fusion, f32[32,20]{0,1:T(8,128)S(1)} %fusion.26), kind=kOutput, calls=%fused_computation.21 | convolution fusion | flops 85360640 | bytes 4101632 | tf_op jit(solution)/shard_map/qhk,khd->qhd/dot_general | solution.py:43
  141.8 0.8 reshape_broadcast_in_dim.3
  (56 shorter events, 7.0 us)
Async XLA Ops:
  7.2 129.0 %all-gather.3.cloned.1.call-start = ((), (), s32[]{:S(2)}) async-start(), calls=%async_computation.4 | async-start | bytes 3932160 | tf_op jit(solution)/shard_map/all_gather | solution.py:96
  10.3 0.9 copy-start.5
  12.7 20.0 %copy-start = (bf16[1,512,1280]{2,1,0:T(8,128)(2,1)S(1)}, bf16[1,512,1280]{2,1,0:T(8,128)(2,1)}, u32[]{:S(2)}) copy-start(bf16[1,512,1280]{2,1,0:T(8,128)(2,1)} %param.16) | copy-start | bytes 3932164
  28.4 43.0 %all-to-all-start.1 = ((bf16[2,2,20480]{2,1,0:T(2,128)(2,1)}), bf16[2,2,20480]{2,1,0:T(2,128)(2,1)S(1)}, u32[]{:S(2)}, u32[]{:S(2)}) async-start(bf16[2,2,20480]{2,1,0:T(2,128)(2,1)} %reshape.109), calls=%async_computation.1 | async-start | bytes 327680 | tf_op jit(solution)/shard_map/all_to_all | solution.py:67
  32.7 106.7 %all-gather.5.cloned.1.call-start = ((), (), s32[]{:S(2)}) async-start(), calls=%async_computation.5 | async-start | bytes 3932160 | tf_op jit(solution)/shard_map/all_gather | solution.py:96
  34.8 0.9 copy-start.3
  34.8 20.1 %copy-start.6 = (bf16[1,32,2560]{2,1,0:T(8,128)(2,1)S(1)}, bf16[1,32,2560]{2,1,0:T(8,128)(2,1)}, u32[]{:S(2)}) copy-start(bf16[1,32,2560]{2,1,0:T(8,128)(2,1)} %param.10) | copy-start | bytes 491524
  55.8 19.7 %copy-start.4 = (bf16[1,64,1280]{2,1,0:T(8,128)(2,1)S(1)}, bf16[1,64,1280]{2,1,0:T(8,128)(2,1)}, u32[]{:S(2)}) copy-start(bf16[1,64,1280]{2,1,0:T(8,128)(2,1)} %param.13) | copy-start | bytes 491524
  70.1 21.5 %copy-start.2 = (bf16[1,32,2560]{2,1,0:T(8,128)(2,1)S(1)}, bf16[1,32,2560]{2,1,0:T(8,128)(2,1)}, u32[]{:S(2)}) copy-start(bf16[1,32,2560]{2,1,0:T(8,128)(2,1)} %param.14) | copy-start | bytes 491524
  71.4 20.3 %copy-start.1 = (bf16[2,2,20480]{2,1,0:T(2,128)(2,1)}, bf16[2,2,20480]{2,1,0:T(2,128)(2,1)S(1)}, u32[]{:S(2)}) copy-start(bf16[2,2,20480]{2,1,0:T(2,128)(2,1)S(1)} %all-to-all-done.1) | copy-start | bytes 491524
  71.4 38.0 %all-to-all-start = ((bf16[2,2,20480]{2,1,0:T(2,128)(2,1)}), bf16[2,2,20480]{2,1,0:T(2,128)(2,1)}, u32[]{:S(2)}, u32[]{:S(2)}) async-start(bf16[2,2,20480]{2,1,0:T(2,128)(2,1)} %reshape.107), calls=%async_computation | async-start | bytes 327680 | tf_op jit(solution)/shard_map/all_to_all | solution.py:68
  92.0 0.9 copy-start.7
  109.4 9.1 %all-to-all-start.2 = ((bf16[2,2,20480]{2,1,0:T(2,128)(2,1)}), bf16[2,2,20480]{2,1,0:T(2,128)(2,1)}, u32[]{:S(2)}, u32[]{:S(2)}) async-start(bf16[2,2,20480]{2,1,0:T(2,128)(2,1)} %reshape.111), calls=%async_computation.2 | async-start | bytes 327680 | tf_op jit(solution)/shard_map/all_to_all | solution.py:69
  124.6 6.0 %copy-start.8 = (s32[1,512]{1,0:T(1,128)S(1)}, s32[1,512]{1,0:T(1,128)}, u32[]{:S(2)}) copy-start(s32[1,512]{1,0:T(1,128)} %param.17) | copy-start | bytes 6148
  127.2 8.1 %all-to-all-start.3 = ((bf16[2,2,20480]{2,1,0:T(2,128)(2,1)}), bf16[2,2,20480]{2,1,0:T(2,128)(2,1)S(1)}, u32[]{:S(2)}, u32[]{:S(2)}) async-start(bf16[2,2,20480]{2,1,0:T(2,128)(2,1)} %reshape.113), calls=%async_computation.3 | async-start | bytes 327680 | tf_op jit(solution)/shard_map/all_to_all | solution.py:108
Sparse Core Ops, SparseCore 0:
  10.4 43.4 all-gather.2
  55.5 40.7 all-gather.4
where the time goes:
time: 150 us; the launch traced here: 149 us
  other arithmetic  45.5 us (30%)
  blocking collectives  35.3 us (24%)
  local copies, waits for them, and re-layouts  27.1 us (18%)
  starting transfers between devices  16 us (11%)
  between operations  14.4 us (10%)
  matrix products  6.43 us (4%)
  waiting for transfers between devices  4.66 us (3%)
    unnamed x4, other arithmetic  44.7 us
    all_gather x1, blocking collectives, per_device(): piece_key = lax.all_gather(stale_key, 'patch', axis=1, tiled=True)  19.2 us
    unnamed x33, local copies, waits for them, and re-layouts  17.3 us
    all_gather x1, blocking collectives, per_device(): piece_value = lax.all_gather(stale_value, 'patch', axis=1, tiled=True)  16.1 us
    all_to_all x1, waiting for transfers between devices, per_device(): lax.all_to_all(self_block, 'head', split_axis=1, concat_axis=2, tiled=True)  4.6 us
    all_to_all x1, starting transfers between devices, per_device(): lax.all_to_all(fresh_value, 'head', split_axis=2, concat_axis=1, tiled=True)  4.28 us
    all_to_all x1, starting transfers between devices, per_device(): lax.all_to_all(fresh_query, 'head', split_axis=2, concat_axis=1, tiled=True)  4.23 us
    all_to_all x1, starting transfers between devices, per_device(): lax.all_to_all(fresh_key, 'head', split_axis=2, concat_axis=1, tiled=True)  4.05 us
  transfers between devices with their start and end apart: 6, of which 1 were waited for; matrix products, arithmetic and copies ran while one was open for 46% of the time, Pallas kernels for 0%

commit v1 on v0

v1 whole, which is shorter than its diff:
```python
import functools
import math

import jax
import jax.numpy as jnp
from jax import lax
from jax.experimental import pallas as pl
from jax.experimental.pallas import tpu as pltpu
from jax.sharding import PartitionSpec as P

HD = 128
MESH = pl.DeviceIdType.MESH


def dot_nt(a, b):
    return lax.dot_general(a, b, (((1,), (1,)), ((), ())), preferred_element_type=jnp.float32)


def kernel(
    n_patch, n_head, nch,
    fq, fk, fv, sk, sv, cq, tk, tv, mask,
    so, co,
    fx, kv, txk, txv, mk, outs, outc,
    x_send, x_recv, x_loc, t_loc, kv_loc, own_send, fwd_send, kv_recv,
    o_send, o_recv, o_loc, c_send, c_recv, c_loc,
):
    p = lax.axis_index("patch")
    h = lax.axis_index("head")
    rows = fq.shape[1]
    prows = rows * n_head
    hcols = sk.shape[2]
    ccols = hcols // nch
    heads = hcols // HD
    cheads = heads // nch
    scale = 1.0 / math.sqrt(HD)
    fresh = (cq, fq, fk, fv)
    my_rows = pl.ds(pl.multiple_of(h * rows, rows), rows)

    for c in range(nch):
        for i, ref in enumerate((sk, sv)):
            pltpu.make_async_copy(
                ref.at[0, :, pl.ds(c * ccols, ccols)], kv.at[p, c, i], kv_loc.at[c, i]
            ).start()
    text_copies = [
        pltpu.make_async_copy(mask, mk, t_loc.at[0]),
        pltpu.make_async_copy(tk.at[0], txk, t_loc.at[1]),
        pltpu.make_async_copy(tv.at[0], txv, t_loc.at[2]),
    ]
    own_copies = [
        pltpu.make_async_copy(
            ref.at[0, :, pl.ds(pl.multiple_of(h * hcols, hcols), hcols)],
            fx.at[a, my_rows, :],
            x_loc.at[a],
        )
        for a, ref in enumerate(fresh)
    ]
    for cp in own_copies + text_copies:
        cp.start()

    barrier = pltpu.get_barrier_semaphore()
    has_right = p < n_patch - 1
    has_left = p > 0

    @pl.when(has_right)
    def _():
        pl.semaphore_signal(barrier, inc=1, device_id={"patch": p + 1}, device_id_type=MESH)

    @pl.when(has_left)
    def _():
        pl.semaphore_signal(barrier, inc=1, device_id={"patch": p - 1}, device_id_type=MESH)

    for k in range(1, n_head):
        pl.semaphore_signal(
            barrier, inc=1, device_id={"head": lax.rem(h + k, n_head)}, device_id_type=MESH
        )
    pl.semaphore_wait(
        barrier, n_head - 1 + has_right.astype(jnp.int32) + has_left.astype(jnp.int32)
    )

    def x_copy(a, k):
        peer = lax.rem(h + k, n_head)
        return pltpu.make_async_remote_copy(
            src_ref=fresh[a].at[0, :, pl.ds(pl.multiple_of(peer * hcols, hcols), hcols)],
            dst_ref=fx.at[a, my_rows, :],
            send_sem=x_send.at[a, k - 1],
            recv_sem=x_recv.at[a, k - 1],
            device_id={"head": peer},
            device_id_type=MESH,
        )

    def kv_copy(src, c, target, sem):
        return pltpu.make_async_remote_copy(
            src_ref=kv.at[src, c],
            dst_ref=kv.at[src, c],
            send_sem=sem,
            recv_sem=kv_recv.at[src, c],
            device_id={"patch": target},
            device_id_type=MESH,
        )

    for a in range(4):
        for k in range(1, n_head):
            x_copy(a, k).start()
    for c in range(nch):
        for i, ref in enumerate((sk, sv)):
            pltpu.make_async_copy(
                ref.at[0, :, pl.ds(c * ccols, ccols)], kv.at[p, c, i], kv_loc.at[c, i]
            ).wait()

        @pl.when(has_right)
        def _():
            kv_copy(p, c, p + 1, own_send.at[0, c]).start()

        @pl.when(has_left)
        def _():
            kv_copy(p, c, p - 1, own_send.at[1, c]).start()

    shorter = jnp.minimum(p, n_patch - 1 - p)

    def slot_source(s):
        near = s // 2 + 1
        near_src = jnp.where(s % 2 == 0, p - near, p + near)
        far = s - shorter + 1
        far_src = jnp.where(p > shorter, p - far, p + far)
        return jnp.where(s < 2 * shorter, near_src, far_src)

    def forward_target(src):
        target = jnp.where(src < p, p + 1, p - 1)
        return target, (target >= 0) & (target < n_patch)

    def forward(s, c):
        src = slot_source(s)
        kv_copy(src, c, p, fwd_send.at[s, c]).wait_recv()
        target, valid = forward_target(src)

        @pl.when(valid)
        def _():
            kv_copy(src, c, target, fwd_send.at[s, c]).start()

    def wait_x(a):
        own_copies[a].wait()
        for k in range(1, n_head):
            x_copy(a, k).wait_recv()

    def out_copy(src, dst, c, k, send, recv):
        peer = lax.rem(h + k, n_head)
        return pltpu.make_async_remote_copy(
            src_ref=src.at[c, pl.ds(pl.multiple_of(peer * rows, rows), rows), :],
            dst_ref=dst.at[0, :, pl.ds(pl.multiple_of(h * hcols + c * ccols, HD), ccols)],
            send_sem=send.at[c, k - 1],
            recv_sem=recv.at[c, k - 1],
            device_id={"head": peer},
            device_id_type=MESH,
        )

    def local_out(src, dst, c, sem):
        return pltpu.make_async_copy(
            src.at[c, my_rows, :],
            dst.at[0, :, pl.ds(pl.multiple_of(h * hcols + c * ccols, HD), ccols)],
            sem.at[c],
        )

    def send_out(src, dst, c, send, recv, loc):
        for k in range(1, n_head):
            out_copy(src, dst, c, k, send, recv).start()
        local_out(src, dst, c, loc).start()

    def cross_chunk(c):
        usable = mk[...] > 0
        for i in range(cheads):
            cols = pl.ds((c * cheads + i) * HD, HD)
            scores = dot_nt(fx[0, :, cols], txk[:, cols]) * scale
            scores = jnp.where(usable, scores, -jnp.inf)
            top = jnp.max(scores, axis=-1, keepdims=True)
            weights = jnp.exp(scores - top)
            total = jnp.sum(weights, axis=-1, keepdims=True)
            mix = jnp.dot(
                weights.astype(jnp.bfloat16), txv[:, cols], preferred_element_type=jnp.float32
            )
            outc[c, :, i * HD : (i + 1) * HD] = (mix / total).astype(jnp.bfloat16)

    def first(j):
        cols = pl.ds(j * HD, HD)
        scores = dot_nt(fx[1, :, cols], fx[2, :, cols]) * scale
        top = jnp.max(scores, axis=-1, keepdims=True)
        weights = jnp.exp(scores - top)
        total = jnp.sum(weights, axis=-1, keepdims=True)
        mix = jnp.dot(
            weights.astype(jnp.bfloat16), fx[3, :, cols], preferred_element_type=jnp.float32
        )
        return top, total, mix

    def absorb(state, src, j):
        top, total, mix = state
        c, i = divmod(j, cheads)
        cols = pl.ds(i * HD, HD)
        scores = dot_nt(fx[1, :, pl.ds(j * HD, HD)], kv[src, c, 0, :, cols]) * scale
        new_top = jnp.maximum(top, jnp.max(scores, axis=-1, keepdims=True))
        weights = jnp.exp(scores - new_top)
        factor = jnp.exp(top - new_top)
        total = total * factor + jnp.sum(weights, axis=-1, keepdims=True)
        mix = mix * factor + jnp.dot(
            weights.astype(jnp.bfloat16), kv[src, c, 1, :, cols],
            preferred_element_type=jnp.float32,
        )
        return new_top, total, mix

    half = (nch + 1) // 2
    for cp in text_copies:
        cp.wait()
    wait_x(0)
    for c in range(half):
        cross_chunk(c)
    for c in range(half):
        forward(0, c)
    for c in range(half, nch):
        cross_chunk(c)
    for c in range(nch):
        send_out(outc, co, c, c_send, c_recv, c_loc)
    for c in range(half, nch):
        forward(0, c)
    for a in range(1, 4):
        wait_x(a)
    states = [first(j) for j in range(heads)]
    src = slot_source(0)
    states = [absorb(states[j], src, j) for j in range(heads)]

    def slot(s, states):
        src = slot_source(s)
        out = []
        for c in range(nch):
            forward(s, c)
            for j in range(c * cheads, (c + 1) * cheads):
                out.append(absorb(states[j], src, j))
        return out

    if n_patch <= 8:
        for s in range(1, n_patch - 2):
            states = slot(s, states)
    else:
        states = lax.fori_loop(1, n_patch - 2, slot, states)
    last = n_patch - 2
    src = slot_source(last)
    for c in range(nch):
        if last > 0:
            forward(last, c)
        for i in range(cheads):
            j = c * cheads + i
            _, total, mix = absorb(states[j], src, j) if last > 0 else states[j]
            outs[c, :, i * HD : (i + 1) * HD] = (mix / total).astype(jnp.bfloat16)
        if c > 0:
            send_out(outs, so, c - 1, o_send, o_recv, o_loc)
    send_out(outs, so, nch - 1, o_send, o_recv, o_loc)

    for c in range(nch):

        @pl.when(has_right)
        def _():
            kv_copy(p, c, p + 1, own_send.at[0, c]).wait_send()

        @pl.when(has_left)
        def _():
            kv_copy(p, c, p - 1, own_send.at[1, c]).wait_send()

    def drain(s, carry):
        for c in range(nch):
            target, valid = forward_target(slot_source(s))

            @pl.when(valid)
            def _():
                kv_copy(slot_source(s), c, target, fwd_send.at[s, c]).wait_send()

        return carry

    if n_patch <= 8:
        for s in range(n_patch - 1):
            drain(s, 0)
    else:
        lax.fori_loop(0, n_patch - 1, drain, 0)
    for a in range(4):
        for k in range(1, n_head):
            x_copy(a, k).wait_send()
    for src_ref, dst, send, recv, loc in (
        (outc, co, c_send, c_recv, c_loc),
        (outs, so, o_send, o_recv, o_loc),
    ):
        for c in range(nch):
            for k in range(1, n_head):
                cp = out_copy(src_ref, dst, c, k, send, recv)
                cp.wait_send()
                cp.wait_recv()
            local_out(src_ref, dst, c, loc).wait()


def per_device(n_patch, n_head, *args):
    fq, fk, fv, sk, sv, cq, tk, tv, mask = args
    rows = fq.shape[1]
    prows = rows * n_head
    hcols = sk.shape[2]
    heads = hcols // HD
    nch = 5 if heads % 5 == 0 else 1
    ccols = hcols // nch
    txt = tk.shape[1]
    peers = max(n_head - 1, 1)
    any_spec = pl.BlockSpec(memory_space=pl.ANY)
    dma = pltpu.SemaphoreType.DMA
    bf16 = jnp.bfloat16
    return pl.pallas_call(
        functools.partial(kernel, n_patch, n_head, nch),
        out_shape=(
            jax.ShapeDtypeStruct(fq.shape, bf16),
            jax.ShapeDtypeStruct(cq.shape, bf16),
        ),
        in_specs=[any_spec] * 9,
        out_specs=(any_spec, any_spec),
        scratch_shapes=[
            pltpu.VMEM((4, prows, hcols), bf16),
            pltpu.VMEM((n_patch, nch, 2, prows, ccols), bf16),
            pltpu.VMEM((txt, hcols), bf16),
            pltpu.VMEM((txt, hcols), bf16),
            pltpu.VMEM((1, txt), jnp.int32),
            pltpu.VMEM((nch, prows, ccols), bf16),
            pltpu.VMEM((nch, prows, ccols), bf16),
            dma((4, peers)),
            dma((4, peers)),
            dma((4,)),
            dma((3,)),
            dma((nch, 2)),
            dma((2, nch)),
            dma((n_patch, nch)),
            dma((n_patch, nch)),
            dma((nch, peers)),
            dma((nch, peers)),
            dma((nch,)),
            dma((nch, peers)),
            dma((nch, peers)),
            dma((nch,)),
        ],
        compiler_params=pltpu.CompilerParams(collective_id=0, has_side_effects=True),
        name="displaced_attention",
    )(*args)


def solution(mesh):
    return jax.shard_map(
        functools.partial(per_device, mesh.shape["patch"], mesh.shape["head"]),
        mesh=mesh,
        in_specs=(
            P(("group", "cfg"), ("patch", "head"), None),
            P(("group", "cfg"), ("patch", "head"), None),
            P(("group", "cfg"), ("patch", "head"), None),
            P(("group", "cfg"), "patch", "head"),
            P(("group", "cfg"), "patch", "head"),
            P(("group", "cfg"), ("patch", "head"), None),
            P(("group", "cfg"), None, "head"),
            P(("group", "cfg"), None, "head"),
            P(("group", "cfg"), None),
        ),
        out_specs=(
            P(("group", "cfg"), ("patch", "head"), None),
            P(("group", "cfg"), ("patch", "head"), None),
        ),
        check_vma=False,
    )
```

time: 150 us -> 40.1 us (0.27)
  other arithmetic: 45.5 us -> 0 us
  Pallas kernels: 0 us -> 36.1 us
  blocking collectives: 35.3 us -> 0 us
  local copies, waits for them, and re-layouts: 27.1 us -> 3.18 us
  starting transfers between devices: 16 us -> 0 us
  between operations: 14.4 us -> 0.64 us
  matrix products: 6.43 us -> 0 us
  waiting for transfers between devices: 4.66 us -> 0 us
    unnamed x4 -> x0, other arithmetic: 44.7 us -> none
    pallas_call x0 -> x1, Pallas kernels: none -> 36.1 us  [per_device(): pl.pallas_call(functools.partial(kernel, n_patch, n_head, nch), out_shape...]
    all_gather x2 -> x0, blocking collectives: 35.3 us -> none  [the longest x1 19.2 us: per_device(): piece_key = lax.all_gather(stale_key, 'patch', axis=1, tiled=True)]
    all_to_all x4 -> x0, starting transfers between devices: 16 us -> none  [the longest x1 4.28 us: per_device(): lax.all_to_all(fresh_value, 'head', split_axis=2, concat_axis=1, tiled=True)]
    unnamed x33 -> x2, local copies, waits for them, and re-layouts: 17.3 us -> 3.18 us
    dot_general x6 -> x0, matrix products: 6.43 us -> none  [the longest x3 3.37 us: scaled_scores(): jnp.einsum('qhd,khd->qhk', queries, key_block, preferred_element_type=jnp...]
    all_to_all x10 -> x0, local copies, waits for them, and re-layouts: 4.93 us -> none  [the longest x3 2.72 us: per_device(): lax.all_to_all(fresh_value, 'head', split_axis=2, concat_axis=1, tiled=True)]
    all_to_all x4 -> x0, waiting for transfers between devices: 4.61 us -> none  [the longest x1 4.6 us: per_device(): lax.all_to_all(self_block, 'head', split_axis=1, concat_axis=2, tiled=True)]
  transfers between devices with their start and end apart: 6 -> 0, of which waited for: 1 -> 0; matrix products, arithmetic and copies ran while one was open for 46% -> 0% of each run, Pallas kernels for 0% -> 0%
where the time goes in v1:
time: 40.1 us; the launch traced here: 39.9 us
  Pallas kernels  36.1 us (90%)
  local copies, waits for them, and re-layouts  3.18 us (8%)
  between operations  0.64 us (2%)
    pallas_call x1, Pallas kernels, per_device(): pl.pallas_call(functools.partial(kernel, n_patch, n_head, nch), out_shape...  36.1 us
    unnamed x2, local copies, waits for them, and re-layouts  3.18 us

profile of v1, /device:TPU:0, one launch (start us, length us, event | category | flops | bytes accessed | tf_op | source)
XLA Modules:
  0.0 39.9 jit_solution(10111902500957811791)
XLA Ops:
  0.6 36.1 %displaced_attention.1 = (bf16[1,32,2560]{2,1,0:T(8,128)(2,1)}, bf16[1,32,2560]{2,1,0:T(8,128)(2,1)}) custom-call(bf16[1,32,2560]{2,1,0:T(8,128)(2,1)} %fq.1, bf16[1,32,2560]{2,1,0:T(8,128)(2,1)} %fk.1, bf16[1,32,2560]{2,1,0:T(8,128)(2,1)} %fv.1, bf16[1,64,1280]{2,1,0:T(8,128)(2,1)} %sk.1, bf16[1,64,1280]{2,1,0:T(8,128)(2,1)} %sv.1, ...), custom_call_target="tpu_custom_call" | custom-call | tf_op jit(solution)/shard_map/displaced_attention/pallas_call | solution.py:308
  36.7 1.6 %copy.13 = bf16[1,32,2560]{2,1,0:T(8,128)(2,1)} copy(bf16[1,32,2560]{2,1,0:T(8,128)(2,1)} %get-tuple-element.4) | data formatting | bytes 327680
  38.3 1.6 %copy.14 = bf16[1,32,2560]{2,1,0:T(8,128)(2,1)} copy(bf16[1,32,2560]{2,1,0:T(8,128)(2,1)} %get-tuple-element.5) | data formatting | bytes 327680

commit v2 on v1

--- a/solution.py
+++ b/solution.py
@@ -292,6 +292,32 @@
             local_out(src_ref, dst, c, loc).wait()
 
 
+def store_kernel(a, b, so, co, sem):
+    copies = [
+        pltpu.make_async_copy(a, so, sem.at[0]),
+        pltpu.make_async_copy(b, co, sem.at[1]),
+    ]
+    for cp in copies:
+        cp.start()
+    for cp in copies:
+        cp.wait()
+
+
+def store(a, b):
+    return pl.pallas_call(
+        store_kernel,
+        out_shape=(
+            jax.ShapeDtypeStruct(a.shape, a.dtype),
+            jax.ShapeDtypeStruct(b.shape, b.dtype),
+        ),
+        in_specs=[pl.BlockSpec(memory_space=pltpu.VMEM)] * 2,
+        out_specs=(pl.BlockSpec(memory_space=pltpu.HBM),) * 2,
+        scratch_shapes=[pltpu.SemaphoreType.DMA((2,))],
+        compiler_params=pltpu.CompilerParams(vmem_limit_bytes=1024 * 1024),
+        name="store_outputs",
+    )(a, b)
+
+
 def per_device(n_patch, n_head, *args):
     fq, fk, fv, sk, sv, cq, tk, tv, mask = args
     rows = fq.shape[1]
@@ -305,14 +331,14 @@
     any_spec = pl.BlockSpec(memory_space=pl.ANY)
     dma = pltpu.SemaphoreType.DMA
     bf16 = jnp.bfloat16
-    return pl.pallas_call(
+    mixed = pl.pallas_call(
         functools.partial(kernel, n_patch, n_head, nch),
         out_shape=(
-            jax.ShapeDtypeStruct(fq.shape, bf16),
-            jax.ShapeDtypeStruct(cq.shape, bf16),
+            pltpu.VMEM(fq.shape, bf16),
+            pltpu.VMEM(cq.shape, bf16),
         ),
         in_specs=[any_spec] * 9,
-        out_specs=(any_spec, any_spec),
+        out_specs=(pl.BlockSpec(memory_space=pltpu.VMEM),) * 2,
         scratch_shapes=[
             pltpu.VMEM((4, prows, hcols), bf16),
             pltpu.VMEM((n_patch, nch, 2, prows, ccols), bf16),
@@ -339,6 +365,7 @@
         compiler_params=pltpu.CompilerParams(collective_id=0, has_side_effects=True),
         name="displaced_attention",
     )(*args)
+    return store(*mixed)
 
 
 def solution(mesh):

time: 40.1 us -> 37.5 us (0.935)
  local copies, waits for them, and re-layouts: 3.18 us -> 0 us
  Pallas kernels: 36.1 us -> 36.7 us
    unnamed x2 -> x0, local copies, waits for them, and re-layouts: 3.18 us -> none
    pallas_call x0 -> x1, Pallas kernels: none -> 0.74 us  [store(): pl.pallas_call(store_kernel, out_shape=(jax.ShapeDtypeStruct(a.shape, a.d...]
where the time goes in v2:
time: 37.5 us; the launch traced here: 37.3 us
  Pallas kernels  36.7 us (98%)
  between operations  0.64 us (2%)
    pallas_call x1, Pallas kernels, per_device(): pl.pallas_call(functools.partial(kernel, n_patch, n_head, nch), out_shape...  36 us

profile of v2, /device:TPU:0, one launch (start us, length us, event | category | flops | bytes accessed | tf_op | source)
XLA Modules:
  0.0 37.3 jit_solution(11075339993852058000)
XLA Ops:
  0.6 36.0 %displaced_attention.1 = (bf16[1,32,2560]{2,1,0:T(8,128)(2,1)S(1)}, bf16[1,32,2560]{2,1,0:T(8,128)(2,1)S(1)}) custom-call(bf16[1,32,2560]{2,1,0:T(8,128)(2,1)} %fq.1, bf16[1,32,2560]{2,1,0:T(8,128)(2,1)} %fk.1, bf16[1,32,2560]{2,1,0:T(8,128)(2,1)} %fv.1, bf16[1,64,1280]{2,1,0:T(8,128)(2,1)} %sk.1, bf16[1,64,1280]{2,1,0:T(8,128)(2,1)} %sv.1, ...), custom_call_target="tpu_custom_call" | custom-call | tf_op jit(solution)/shard_map/displaced_attention/pallas_call | solution.py:334
  36.6 0.7 %store_outputs.1 = (bf16[1,32,2560]{2,1,0:T(8,128)(2,1)}, bf16[1,32,2560]{2,1,0:T(8,128)(2,1)}) custom-call(bf16[1,32,2560]{2,1,0:T(8,128)(2,1)S(1)} %get-tuple-element.4.a, bf16[1,32,2560]{2,1,0:T(8,128)(2,1)S(1)} %get-tuple-element.5.b), custom_call_target="tpu_custom_call" | custom-call | tf_op jit(solution)/shard_map/store_outputs/pallas_call | solution.py:307

commit v3 on v2

--- a/solution.py
+++ b/solution.py
@@ -23,6 +23,7 @@
     fx, kv, txk, txv, mk, outs, outc,
     x_send, x_recv, x_loc, t_loc, kv_loc, own_send, fwd_send, kv_recv,
     o_send, o_recv, o_loc, c_send, c_recv, c_loc,
+    dq, part_out, part_in, stat_out, stat_in, dq_sem, part_send, part_recv,
 ):
     p = lax.axis_index("patch")
     h = lax.axis_index("head")
@@ -98,44 +99,15 @@
             device_id_type=MESH,
         )
 
-    for a in range(4):
+    for a in (1, 0, 2, 3):
         for k in range(1, n_head):
             x_copy(a, k).start()
-    for c in range(nch):
+
+    def wait_own_kv(c):
         for i, ref in enumerate((sk, sv)):
             pltpu.make_async_copy(
                 ref.at[0, :, pl.ds(c * ccols, ccols)], kv.at[p, c, i], kv_loc.at[c, i]
             ).wait()
-
-        @pl.when(has_right)
-        def _():
-            kv_copy(p, c, p + 1, own_send.at[0, c]).start()
-
-        @pl.when(has_left)
-        def _():
-            kv_copy(p, c, p - 1, own_send.at[1, c]).start()
-
-    shorter = jnp.minimum(p, n_patch - 1 - p)
-
-    def slot_source(s):
-        near = s // 2 + 1
-        near_src = jnp.where(s % 2 == 0, p - near, p + near)
-        far = s - shorter + 1
-        far_src = jnp.where(p > shorter, p - far, p + far)
-        return jnp.where(s < 2 * shorter, near_src, far_src)
-
-    def forward_target(src):
-        target = jnp.where(src < p, p + 1, p - 1)
-        return target, (target >= 0) & (target < n_patch)
-
-    def forward(s, c):
-        src = slot_source(s)
-        kv_copy(src, c, p, fwd_send.at[s, c]).wait_recv()
-        target, valid = forward_target(src)
-
-        @pl.when(valid)
-        def _():
-            kv_copy(src, c, target, fwd_send.at[s, c]).start()
 
     def wait_x(a):
         own_copies[a].wait()
@@ -181,20 +153,27 @@
 
     def first(j):
         cols = pl.ds(j * HD, HD)
-        scores = dot_nt(fx[1, :, cols], fx[2, :, cols]) * scale
+        return start(fx[1, :, cols], fx[2, :, cols], fx[3, :, cols])
+
+    def start(q, keys, values):
+        scores = dot_nt(q, keys) * scale
         top = jnp.max(scores, axis=-1, keepdims=True)
         weights = jnp.exp(scores - top)
         total = jnp.sum(weights, axis=-1, keepdims=True)
         mix = jnp.dot(
-            weights.astype(jnp.bfloat16), fx[3, :, cols], preferred_element_type=jnp.float32
+            weights.astype(jnp.bfloat16), values, preferred_element_type=jnp.float32
         )
         return top, total, mix
 
-    def absorb(state, src, j):
+    def query(j):
+        return fx[1, :, pl.ds(j * HD, HD)]
+
+    def absorb(state, src, j, q=None):
         top, total, mix = state
         c, i = divmod(j, cheads)
         cols = pl.ds(i * HD, HD)
-        scores = dot_nt(fx[1, :, pl.ds(j * HD, HD)], kv[src, c, 0, :, cols]) * scale
+        q = query(j) if q is None else q
+        scores = dot_nt(q, kv[src, c, 0, :, cols]) * scale
         new_top = jnp.maximum(top, jnp.max(scores, axis=-1, keepdims=True))
         weights = jnp.exp(scores - new_top)
         factor = jnp.exp(top - new_top)
@@ -205,78 +184,248 @@
         )
         return new_top, total, mix
 
-    half = (nch + 1) // 2
-    for cp in text_copies:
-        cp.wait()
-    wait_x(0)
-    for c in range(half):
-        cross_chunk(c)
-    for c in range(half):
-        forward(0, c)
-    for c in range(half, nch):
-        cross_chunk(c)
-    for c in range(nch):
-        send_out(outc, co, c, c_send, c_recv, c_loc)
-    for c in range(half, nch):
-        forward(0, c)
-    for a in range(1, 4):
-        wait_x(a)
-    states = [first(j) for j in range(heads)]
-    src = slot_source(0)
-    states = [absorb(states[j], src, j) for j in range(heads)]
-
-    def slot(s, states):
-        src = slot_source(s)
-        out = []
-        for c in range(nch):
-            forward(s, c)
-            for j in range(c * cheads, (c + 1) * cheads):
-                out.append(absorb(states[j], src, j))
-        return out
-
-    if n_patch <= 8:
-        for s in range(1, n_patch - 2):
-            states = slot(s, states)
-    else:
-        states = lax.fori_loop(1, n_patch - 2, slot, states)
-    last = n_patch - 2
-    src = slot_source(last)
-    for c in range(nch):
-        if last > 0:
-            forward(last, c)
-        for i in range(cheads):
-            j = c * cheads + i
-            _, total, mix = absorb(states[j], src, j) if last > 0 else states[j]
-            outs[c, :, i * HD : (i + 1) * HD] = (mix / total).astype(jnp.bfloat16)
-        if c > 0:
-            send_out(outs, so, c - 1, o_send, o_recv, o_loc)
-    send_out(outs, so, nch - 1, o_send, o_recv, o_loc)
-
-    for c in range(nch):
-
-        @pl.when(has_right)
-        def _():
-            kv_copy(p, c, p + 1, own_send.at[0, c]).wait_send()
-
-        @pl.when(has_left)
-        def _():
-            kv_copy(p, c, p - 1, own_send.at[1, c]).wait_send()
-
-    def drain(s, carry):
-        for c in range(nch):
-            target, valid = forward_target(slot_source(s))
+    def line_program():
+        for c in range(nch):
+            wait_own_kv(c)
+
+            @pl.when(has_right)
+            def _():
+                kv_copy(p, c, p + 1, own_send.at[0, c]).start()
+
+            @pl.when(has_left)
+            def _():
+                kv_copy(p, c, p - 1, own_send.at[1, c]).start()
+
+        shorter = jnp.minimum(p, n_patch - 1 - p)
+
+        def slot_source(s):
+            near = s // 2 + 1
+            near_src = jnp.where(s % 2 == 0, p - near, p + near)
+            far = s - shorter + 1
+            far_src = jnp.where(p > shorter, p - far, p + far)
+            return jnp.where(s < 2 * shorter, near_src, far_src)
+
+        def forward_target(src):
+            target = jnp.where(src < p, p + 1, p - 1)
+            return target, (target >= 0) & (target < n_patch)
+
+        def forward(s, c):
+            src = slot_source(s)
+            kv_copy(src, c, p, fwd_send.at[s, c]).wait_recv()
+            target, valid = forward_target(src)
 
             @pl.when(valid)
             def _():
-                kv_copy(slot_source(s), c, target, fwd_send.at[s, c]).wait_send()
-
-        return carry
-
-    if n_patch <= 8:
-        for s in range(n_patch - 1):
-            drain(s, 0)
+                kv_copy(src, c, target, fwd_send.at[s, c]).start()
+
+        half = (nch + 1) // 2
+        for cp in text_copies:
+            cp.wait()
+        wait_x(0)
+        for c in range(half):
+            cross_chunk(c)
+        for c in range(half):
+            forward(0, c)
+        for c in range(half, nch):
+            cross_chunk(c)
+        for c in range(nch):
+            send_out(outc, co, c, c_send, c_recv, c_loc)
+        for c in range(half, nch):
+            forward(0, c)
+        for a in range(1, 4):
+            wait_x(a)
+        states = [first(j) for j in range(heads)]
+        src = slot_source(0)
+        states = [absorb(states[j], src, j) for j in range(heads)]
+
+        def slot(s, states):
+            src = slot_source(s)
+            out = []
+            for c in range(nch):
+                forward(s, c)
+                for j in range(c * cheads, (c + 1) * cheads):
+                    out.append(absorb(states[j], src, j))
+            return out
+
+        if n_patch <= 8:
+            for s in range(1, n_patch - 2):
+                states = slot(s, states)
+        else:
+            states = lax.fori_loop(1, n_patch - 2, slot, states)
+        last = n_patch - 2
+        src = slot_source(last)
+        for c in range(nch):
+            if last > 0:
+                forward(last, c)
+            for i in range(cheads):
+                j = c * cheads + i
+                _, total, mix = absorb(states[j], src, j) if last > 0 else states[j]
+                outs[c, :, i * HD : (i + 1) * HD] = (mix / total).astype(jnp.bfloat16)
+            if c > 0:
+                send_out(outs, so, c - 1, o_send, o_recv, o_loc)
+        send_out(outs, so, nch - 1, o_send, o_recv, o_loc)
+
+        for c in range(nch):
+
+            @pl.when(has_right)
+            def _():
+                kv_copy(p, c, p + 1, own_send.at[0, c]).wait_send()
+
+            @pl.when(has_left)
+            def _():
+                kv_copy(p, c, p - 1, own_send.at[1, c]).wait_send()
+
+        def drain(s, carry):
+            for c in range(nch):
+                target, valid = forward_target(slot_source(s))
+
+                @pl.when(valid)
+                def _():
+                    kv_copy(slot_source(s), c, target, fwd_send.at[s, c]).wait_send()
+
+            return carry
+
+        if n_patch <= 8:
+            for s in range(n_patch - 1):
+                drain(s, 0)
+        else:
+            lax.fori_loop(0, n_patch - 1, drain, 0)
+
+    is_end = jnp.logical_not(has_right & has_left)
+    across = n_patch - 1 - p
+    lanes = lax.broadcasted_iota(jnp.int32, (prows, HD), 1)
+
+    def neighbour(c, other):
+        return [
+            pltpu.make_async_remote_copy(
+                src_ref=src.at[c],
+                dst_ref=dst.at[c],
+                send_sem=part_send.at[c, i],
+                recv_sem=part_recv.at[c, i],
+                device_id={"patch": other},
+                device_id_type=MESH,
+            )
+            for i, (src, dst) in enumerate(((part_out, part_in), (stat_out, stat_in)))
+        ]
+
+    def dq_copy(other):
+        return pltpu.make_async_remote_copy(
+            src_ref=fx.at[1],
+            dst_ref=dq,
+            send_sem=dq_sem.at[0],
+            recv_sem=dq_sem.at[1],
+            device_id={"patch": other},
+            device_id_type=MESH,
+        )
+
+    def end_program():
+        helper = jnp.where(has_right, p + 1, p - 1)
+        lead = min(2, nch)
+        for c in range(lead):
+            wait_own_kv(c)
+            kv_copy(p, c, helper, own_send.at[0, c]).start()
+        wait_x(1)
+        dq_copy(helper).start()
+        for c in range(lead, nch):
+            wait_own_kv(c)
+            kv_copy(p, c, helper, own_send.at[0, c]).start()
+        for cp in text_copies:
+            cp.wait()
+        wait_x(0)
+        for c in range(nch):
+            cross_chunk(c)
+            if c > 0:
+                send_out(outc, co, c - 1, c_send, c_recv, c_loc)
+        send_out(outc, co, nch - 1, c_send, c_recv, c_loc)
+        wait_x(2)
+        wait_x(3)
+        states = [first(j) for j in range(heads)]
+        for c in range(nch):
+            for cp in neighbour(c, helper):
+                cp.wait_recv()
+            for i in range(cheads):
+                top, total, mix = states[c * cheads + i]
+                cols = slice(i * HD, (i + 1) * HD)
+                lse = stat_in[c, :, i : i + 1]
+                new_top = jnp.maximum(top, lse)
+                mine = jnp.exp(top - new_top)
+                theirs = jnp.exp(lse - new_top)
+                mix = mix * mine + part_in[c, :, cols].astype(jnp.float32) * theirs
+                outs[c, :, cols] = (mix / (total * mine + theirs)).astype(jnp.bfloat16)
+            send_out(outs, so, c, o_send, o_recv, o_loc)
+        for c in range(nch):
+            kv_copy(p, c, helper, own_send.at[0, c]).wait_send()
+        dq_copy(helper).wait_send()
+
+    def helper_program():
+        end = jnp.where(p < across, p - 1, p + 1)
+        far = n_patch - 1 - end
+        for c in range(nch):
+            wait_own_kv(c)
+            kv_copy(p, c, across, own_send.at[0, c]).start()
+
+        def pass_on(c):
+            kv_copy(end, c, across, fwd_send.at[0, c]).wait_recv()
+            kv_copy(end, c, across, fwd_send.at[0, c]).start()
+
+        pass_on(0)
+        for cp in text_copies:
+            cp.wait()
+        wait_x(0)
+        for c in range(nch):
+            cross_chunk(c)
+            if c > 0:
+                send_out(outc, co, c - 1, c_send, c_recv, c_loc)
+            if c + 1 < nch:
+                pass_on(c + 1)
+        send_out(outc, co, nch - 1, c_send, c_recv, c_loc)
+        for a in range(1, 4):
+            wait_x(a)
+        dq_copy(end).wait_recv()
+
+        def both(j):
+            return jnp.concatenate([query(j), dq[:, pl.ds(j * HD, HD)]], axis=0)
+
+        states = []
+        for j in range(heads):
+            c, i = divmod(j, cheads)
+            cols = pl.ds(i * HD, HD)
+            mine = absorb(first(j), end, j)
+            theirs = start(
+                dq[:, pl.ds(j * HD, HD)], kv[p, c, 0, :, cols], kv[p, c, 1, :, cols]
+            )
+            states.append([jnp.concatenate(pair, axis=0) for pair in zip(mine, theirs)])
+        for c in range(nch):
+            kv_copy(across, c, p, own_send.at[0, c]).wait_recv()
+            for j in range(c * cheads, (c + 1) * cheads):
+                states[j] = absorb(states[j], across, j, both(j))
+        for c in range(nch):
+            kv_copy(far, c, p, own_send.at[0, c]).wait_recv()
+            stat = jnp.zeros((prows, HD), jnp.float32)
+            for i in range(cheads):
+                j = c * cheads + i
+                top, total, mix = absorb(states[j], far, j, both(j))
+                mixed = (mix / total).astype(jnp.bfloat16)
+                lse = top[prows:] + jnp.log(total[prows:])
+                stat = jnp.where(lanes == i, lse, stat)
+                part_out[c, :, i * HD : (i + 1) * HD] = mixed[prows:]
+                outs[c, :, i * HD : (i + 1) * HD] = mixed[:prows]
+            stat_out[c] = stat
+            for cp in neighbour(c, end):
+                cp.start()
+            send_out(outs, so, c, o_send, o_recv, o_loc)
+        for c in range(nch):
+            kv_copy(p, c, across, own_send.at[0, c]).wait_send()
+            kv_copy(end, c, across, fwd_send.at[0, c]).wait_send()
+            for cp in neighbour(c, end):
+                cp.wait_send()
+
+    if n_patch == 4:
+        pl.when(is_end)(end_program)
+        pl.when(jnp.logical_not(is_end))(helper_program)
     else:
-        lax.fori_loop(0, n_patch - 1, drain, 0)
+        line_program()
+
     for a in range(4):
         for k in range(1, n_head):
             x_copy(a, k).wait_send()
@@ -361,6 +510,14 @@
             dma((nch, peers)),
             dma((nch, peers)),
             dma((nch,)),
+            pltpu.VMEM((prows, hcols), bf16),
+            pltpu.VMEM((nch, prows, ccols), bf16),
+            pltpu.VMEM((nch, prows, ccols), bf16),
+            pltpu.VMEM((nch, prows, HD), jnp.float32),
+            pltpu.VMEM((nch, prows, HD), jnp.float32),
+            dma((2,)),
+            dma((nch, 2)),
+            dma((nch, 2)),
         ],
         compiler_params=pltpu.CompilerParams(collective_id=0, has_side_effects=True),
         name="displaced_attention",

time: 37.5 us -> 38.2 us (1.019)
  Pallas kernels: 36.7 us -> 37.4 us
    pallas_call x1, Pallas kernels: 36 us -> 36.6 us  [per_device(): pl.pallas_call(functools.partial(kernel, n_patch, n_head, nch), out_shape...]
where the time goes in v3:
time: 38.2 us; the launch traced here: 38 us
  Pallas kernels  37.4 us (98%)
  between operations  0.64 us (2%)
    pallas_call x1, Pallas kernels, per_device(): pl.pallas_call(functools.partial(kernel, n_patch, n_head, nch), out_shape...  36.6 us

profile of v3, /device:TPU:0, one launch (start us, length us, event | category | flops | bytes accessed | tf_op | source)
XLA Modules:
  0.0 38.0 jit_solution(8477223096844701011)
XLA Ops:
  0.6 36.6 %displaced_attention.1 = (bf16[1,32,2560]{2,1,0:T(8,128)(2,1)S(1)}, bf16[1,32,2560]{2,1,0:T(8,128)(2,1)S(1)}) custom-call(bf16[1,32,2560]{2,1,0:T(8,128)(2,1)} %fq.1, bf16[1,32,2560]{2,1,0:T(8,128)(2,1)} %fk.1, bf16[1,32,2560]{2,1,0:T(8,128)(2,1)} %fv.1, bf16[1,64,1280]{2,1,0:T(8,128)(2,1)} %sk.1, bf16[1,64,1280]{2,1,0:T(8,128)(2,1)} %sv.1, ...), custom_call_target="tpu_custom_call" | custom-call | tf_op jit(solution)/shard_map/displaced_attention/pallas_call | solution.py:483
  37.3 0.7 %store_outputs.1 = (bf16[1,32,2560]{2,1,0:T(8,128)(2,1)}, bf16[1,32,2560]{2,1,0:T(8,128)(2,1)}) custom-call(bf16[1,32,2560]{2,1,0:T(8,128)(2,1)S(1)} %get-tuple-element.4.a, bf16[1,32,2560]{2,1,0:T(8,128)(2,1)S(1)} %get-tuple-element.5.b), custom_call_target="tpu_custom_call" | custom-call | tf_op jit(solution)/shard_map/store_outputs/pallas_call | solution.py:456

commit v4 on v3

--- a/solution.py
+++ b/solution.py
@@ -151,38 +151,38 @@
             )
             outc[c, :, i * HD : (i + 1) * HD] = (mix / total).astype(jnp.bfloat16)
 
-    def first(j):
-        cols = pl.ds(j * HD, HD)
-        return start(fx[1, :, cols], fx[2, :, cols], fx[3, :, cols])
-
-    def start(q, keys, values):
-        scores = dot_nt(q, keys) * scale
-        top = jnp.max(scores, axis=-1, keepdims=True)
-        weights = jnp.exp(scores - top)
-        total = jnp.sum(weights, axis=-1, keepdims=True)
-        mix = jnp.dot(
-            weights.astype(jnp.bfloat16), values, preferred_element_type=jnp.float32
-        )
-        return top, total, mix
-
     def query(j):
         return fx[1, :, pl.ds(j * HD, HD)]
 
-    def absorb(state, src, j, q=None):
+    def weigh(q, keys, values, top=None):
+        scores = dot_nt(q, keys) * scale
+        new_top = jnp.max(scores, axis=-1, keepdims=True)
+        if top is not None:
+            new_top = jnp.maximum(top, new_top)
+        weights = jnp.exp(scores - new_top).astype(jnp.bfloat16)
+        wide = jnp.concatenate([values, jnp.ones_like(values)], axis=1)
+        mixed = jnp.dot(weights, wide, preferred_element_type=jnp.float32)
+        return new_top, mixed[:, HD:], mixed[:, :HD]
+
+    def absorb_rows(state, q, keys, values):
         top, total, mix = state
-        c, i = divmod(j, cheads)
-        cols = pl.ds(i * HD, HD)
-        q = query(j) if q is None else q
-        scores = dot_nt(q, kv[src, c, 0, :, cols]) * scale
-        new_top = jnp.maximum(top, jnp.max(scores, axis=-1, keepdims=True))
-        weights = jnp.exp(scores - new_top)
+        new_top, more_total, more_mix = weigh(q, keys, values, top)
         factor = jnp.exp(top - new_top)
-        total = total * factor + jnp.sum(weights, axis=-1, keepdims=True)
-        mix = mix * factor + jnp.dot(
-            weights.astype(jnp.bfloat16), kv[src, c, 1, :, cols],
-            preferred_element_type=jnp.float32,
-        )
-        return new_top, total, mix
+        return new_top, total * factor + more_total, mix * factor + more_mix
+
+    def kv_rows(i, j, *sources):
+        c, k = divmod(j, cheads)
+        parts = [kv[src, c, i, :, pl.ds(k * HD, HD)] for src in sources]
+        return parts[0] if len(parts) == 1 else jnp.concatenate(parts, axis=0)
+
+    def fresh_rows(i, j):
+        return fx[2 + i, :, pl.ds(j * HD, HD)]
+
+    def first(j):
+        return weigh(query(j), fresh_rows(0, j), fresh_rows(1, j))
+
+    def absorb(state, src, j):
+        return absorb_rows(state, query(j), kv_rows(0, j, src), kv_rows(1, j, src))
 
     def line_program():
         for c in range(nch):
@@ -388,23 +388,23 @@
 
         states = []
         for j in range(heads):
-            c, i = divmod(j, cheads)
-            cols = pl.ds(i * HD, HD)
-            mine = absorb(first(j), end, j)
-            theirs = start(
-                dq[:, pl.ds(j * HD, HD)], kv[p, c, 0, :, cols], kv[p, c, 1, :, cols]
+            mine = weigh(
+                query(j),
+                jnp.concatenate([fresh_rows(0, j), kv_rows(0, j, end)], axis=0),
+                jnp.concatenate([fresh_rows(1, j), kv_rows(1, j, end)], axis=0),
             )
+            theirs = weigh(dq[:, pl.ds(j * HD, HD)], kv_rows(0, j, p), kv_rows(1, j, p))
             states.append([jnp.concatenate(pair, axis=0) for pair in zip(mine, theirs)])
         for c in range(nch):
             kv_copy(across, c, p, own_send.at[0, c]).wait_recv()
-            for j in range(c * cheads, (c + 1) * cheads):
-                states[j] = absorb(states[j], across, j, both(j))
         for c in range(nch):
             kv_copy(far, c, p, own_send.at[0, c]).wait_recv()
             stat = jnp.zeros((prows, HD), jnp.float32)
             for i in range(cheads):
                 j = c * cheads + i
-                top, total, mix = absorb(states[j], far, j, both(j))
+                top, total, mix = absorb_rows(
+                    states[j], both(j), kv_rows(0, j, across, far), kv_rows(1, j, across, far)
+                )
                 mixed = (mix / total).astype(jnp.bfloat16)
                 lse = top[prows:] + jnp.log(total[prows:])
                 stat = jnp.where(lanes == i, lse, stat)

time: 38.2 us -> 32.5 us (0.85)
  Pallas kernels: 37.4 us -> 31.7 us
    pallas_call x1, Pallas kernels: 36.6 us -> 30.9 us  [per_device(): pl.pallas_call(functools.partial(kernel, n_patch, n_head, nch), out_shape...]
where the time goes in v4:
time: 32.5 us; the launch traced here: 32.3 us
  Pallas kernels  31.7 us (98%)
  between operations  0.64 us (2%)
    pallas_call x1, Pallas kernels, per_device(): pl.pallas_call(functools.partial(kernel, n_patch, n_head, nch), out_shape...  30.9 us
    pallas_call x1, Pallas kernels, store(): pl.pallas_call(store_kernel, out_shape=(jax.ShapeDtypeStruct(a.shape, a.d...  0.74 us

profile of v4, /device:TPU:0, one launch (start us, length us, event | category | flops | bytes accessed | tf_op | source)
XLA Modules:
  0.0 32.3 jit_solution(2039950367953212015)
XLA Ops:
  0.6 30.9 %displaced_attention.1 = (bf16[1,32,2560]{2,1,0:T(8,128)(2,1)S(1)}, bf16[1,32,2560]{2,1,0:T(8,128)(2,1)S(1)}) custom-call(bf16[1,32,2560]{2,1,0:T(8,128)(2,1)} %fq.1, bf16[1,32,2560]{2,1,0:T(8,128)(2,1)} %fk.1, bf16[1,32,2560]{2,1,0:T(8,128)(2,1)} %fv.1, bf16[1,64,1280]{2,1,0:T(8,128)(2,1)} %sk.1, bf16[1,64,1280]{2,1,0:T(8,128)(2,1)} %sv.1, ...), custom_call_target="tpu_custom_call" | custom-call | tf_op jit(solution)/shard_map/displaced_attention/pallas_call | solution.py:483
  31.6 0.7 %store_outputs.1 = (bf16[1,32,2560]{2,1,0:T(8,128)(2,1)}, bf16[1,32,2560]{2,1,0:T(8,128)(2,1)}) custom-call(bf16[1,32,2560]{2,1,0:T(8,128)(2,1)S(1)} %get-tuple-element.4.a, bf16[1,32,2560]{2,1,0:T(8,128)(2,1)S(1)} %get-tuple-element.5.b), custom_call_target="tpu_custom_call" | custom-call | tf_op jit(solution)/shard_map/store_outputs/pallas_call | solution.py:456

commit v5 on v4

--- a/solution.py
+++ b/solution.py
@@ -99,9 +99,10 @@
             device_id_type=MESH,
         )
 
-    for a in (1, 0, 2, 3):
-        for k in range(1, n_head):
-            x_copy(a, k).start()
+    def start_x():
+        for a in (1, 0, 2, 3):
+            for k in range(1, n_head):
+                x_copy(a, k).start()
 
     def wait_own_kv(c):
         for i, ref in enumerate((sk, sv)):
@@ -185,6 +186,7 @@
         return absorb_rows(state, query(j), kv_rows(0, j, src), kv_rows(1, j, src))
 
     def line_program():
+        start_x()
         for c in range(nch):
             wait_own_kv(c)
 
@@ -324,6 +326,7 @@
         for c in range(lead):
             wait_own_kv(c)
             kv_copy(p, c, helper, own_send.at[0, c]).start()
+        start_x()
         wait_x(1)
         dq_copy(helper).start()
         for c in range(lead, nch):
@@ -363,6 +366,8 @@
         for c in range(nch):
             wait_own_kv(c)
             kv_copy(p, c, across, own_send.at[0, c]).start()
+
+        start_x()
 
         def pass_on(c):
             kv_copy(end, c, across, fwd_send.at[0, c]).wait_recv()
@@ -473,7 +478,7 @@
     prows = rows * n_head
     hcols = sk.shape[2]
     heads = hcols // HD
-    nch = 5 if heads % 5 == 0 else 1
+    nch = 2 if heads % 2 == 0 else 1
     ccols = hcols // nch
     txt = tk.shape[1]
     peers = max(n_head - 1, 1)

time: 32.5 us -> 31.8 us (0.978)
  Pallas kernels: 31.7 us -> 31 us
    pallas_call x1, Pallas kernels: 30.9 us -> 30.3 us  [per_device(): pl.pallas_call(functools.partial(kernel, n_patch, n_head, nch), out_shape...]
where the time goes in v5:
time: 31.8 us; the launch traced here: 31.6 us
  Pallas kernels  31 us (97%)
  between operations  0.64 us (2%)
    pallas_call x1, Pallas kernels, per_device(): pl.pallas_call(functools.partial(kernel, n_patch, n_head, nch), out_shape...  30.3 us
    pallas_call x1, Pallas kernels, store(): pl.pallas_call(store_kernel, out_shape=(jax.ShapeDtypeStruct(a.shape, a.d...  0.74 us

profile of v5, /device:TPU:0, one launch (start us, length us, event | category | flops | bytes accessed | tf_op | source)
XLA Modules:
  0.0 31.6 jit_solution(8902287562244431443)
XLA Ops:
  0.6 30.3 %displaced_attention.1 = (bf16[1,32,2560]{2,1,0:T(8,128)(2,1)S(1)}, bf16[1,32,2560]{2,1,0:T(8,128)(2,1)S(1)}) custom-call(bf16[1,32,2560]{2,1,0:T(8,128)(2,1)} %fq.1, bf16[1,32,2560]{2,1,0:T(8,128)(2,1)} %fk.1, bf16[1,32,2560]{2,1,0:T(8,128)(2,1)} %fv.1, bf16[1,64,1280]{2,1,0:T(8,128)(2,1)} %sk.1, bf16[1,64,1280]{2,1,0:T(8,128)(2,1)} %sv.1, ...), custom_call_target="tpu_custom_call" | custom-call | tf_op jit(solution)/shard_map/displaced_attention/pallas_call | solution.py:488
  30.9 0.7 %store_outputs.1 = (bf16[1,32,2560]{2,1,0:T(8,128)(2,1)}, bf16[1,32,2560]{2,1,0:T(8,128)(2,1)}) custom-call(bf16[1,32,2560]{2,1,0:T(8,128)(2,1)S(1)} %get-tuple-element.4.a, bf16[1,32,2560]{2,1,0:T(8,128)(2,1)S(1)} %get-tuple-element.5.b), custom_call_target="tpu_custom_call" | custom-call | tf_op jit(solution)/shard_map/store_outputs/pallas_call | solution.py:461

commit v6 on v5

--- a/solution.py
+++ b/solution.py
@@ -297,17 +297,25 @@
     across = n_patch - 1 - p
     lanes = lax.broadcasted_iota(jnp.int32, (prows, HD), 1)
 
+    early = (cheads + 1) // 2
+
     def neighbour(c, other):
         return [
             pltpu.make_async_remote_copy(
-                src_ref=src.at[c],
-                dst_ref=dst.at[c],
+                src_ref=src.at[c, :, pl.ds(at, size)],
+                dst_ref=dst.at[c, :, pl.ds(at, size)],
                 send_sem=part_send.at[c, i],
                 recv_sem=part_recv.at[c, i],
                 device_id={"patch": other},
                 device_id_type=MESH,
             )
-            for i, (src, dst) in enumerate(((part_out, part_in), (stat_out, stat_in)))
+            for i, (src, dst, at, size) in enumerate(
+                (
+                    (part_out, part_in, 0, early * HD),
+                    (part_out, part_in, early * HD, (cheads - early) * HD),
+                    (stat_out, stat_in, 0, HD),
+                )
+            )
         ]
 
     def dq_copy(other):
@@ -415,8 +423,10 @@
                 stat = jnp.where(lanes == i, lse, stat)
                 part_out[c, :, i * HD : (i + 1) * HD] = mixed[prows:]
                 outs[c, :, i * HD : (i + 1) * HD] = mixed[:prows]
+                if i == early - 1:
+                    neighbour(c, end)[0].start()
             stat_out[c] = stat
-            for cp in neighbour(c, end):
+            for cp in neighbour(c, end)[1:]:
                 cp.start()
             send_out(outs, so, c, o_send, o_recv, o_loc)
         for c in range(nch):
@@ -521,8 +531,8 @@
             pltpu.VMEM((nch, prows, HD), jnp.float32),
             pltpu.VMEM((nch, prows, HD), jnp.float32),
             dma((2,)),
-            dma((nch, 2)),
-            dma((nch, 2)),
+            dma((nch, 3)),
+            dma((nch, 3)),
         ],
         compiler_params=pltpu.CompilerParams(collective_id=0, has_side_effects=True),
         name="displaced_attention",

time: 31.8 us -> 31.2 us (0.981)
  Pallas kernels: 31 us -> 30.4 us
    pallas_call x1, Pallas kernels: 30.3 us -> 29.7 us  [per_device(): pl.pallas_call(functools.partial(kernel, n_patch, n_head, nch), out_shape...]
where the time goes in v6:
time: 31.2 us; the launch traced here: 31.1 us
  Pallas kernels  30.4 us (97%)
  between operations  0.64 us (2%)
    pallas_call x1, Pallas kernels, per_device(): pl.pallas_call(functools.partial(kernel, n_patch, n_head, nch), out_shape...  29.7 us
    pallas_call x1, Pallas kernels, store(): pl.pallas_call(store_kernel, out_shape=(jax.ShapeDtypeStruct(a.shape, a.d...  0.74 us

profile of v6, /device:TPU:0, one launch (start us, length us, event | category | flops | bytes accessed | tf_op | source)
XLA Modules:
  0.0 31.1 jit_solution(3708170898712100400)
XLA Ops:
  0.6 29.7 %displaced_attention.1 = (bf16[1,32,2560]{2,1,0:T(8,128)(2,1)S(1)}, bf16[1,32,2560]{2,1,0:T(8,128)(2,1)S(1)}) custom-call(bf16[1,32,2560]{2,1,0:T(8,128)(2,1)} %fq.1, bf16[1,32,2560]{2,1,0:T(8,128)(2,1)} %fk.1, bf16[1,32,2560]{2,1,0:T(8,128)(2,1)} %fv.1, bf16[1,64,1280]{2,1,0:T(8,128)(2,1)} %sk.1, bf16[1,64,1280]{2,1,0:T(8,128)(2,1)} %sv.1, ...), custom_call_target="tpu_custom_call" | custom-call | tf_op jit(solution)/shard_map/displaced_attention/pallas_call | solution.py:498
  30.3 0.7 %store_outputs.1 = (bf16[1,32,2560]{2,1,0:T(8,128)(2,1)}, bf16[1,32,2560]{2,1,0:T(8,128)(2,1)}) custom-call(bf16[1,32,2560]{2,1,0:T(8,128)(2,1)S(1)} %get-tuple-element.4.a, bf16[1,32,2560]{2,1,0:T(8,128)(2,1)S(1)} %get-tuple-element.5.b), custom_call_target="tpu_custom_call" | custom-call | tf_op jit(solution)/shard_map/store_outputs/pallas_call | solution.py:471
